TPU v7x, 32 devices: a whole 2x2x4 slice. The times are simulated.
32 devices in a mesh: parts: 2 (over y), blk: 4 (over z), grp: 4 (over x, core).
Axes of the slice: x: 2, y: 2, z: 4, core: 2. Of those that a mesh axis runs over, the one named last changes fastest.
Arguments:
- factors: float32 [64, 4096], P(None, ('parts', 'blk', 'grp')), parts along dimension 1, may hold values from -1 to 1
- tangent: float32 [64, 4096], P(None, ('parts', 'blk', 'grp')), parts along dimension 1, may hold values from -15 to 15
- counts: int32 [4096, 2048], P(('parts', 'blk', 'grp')), parts along dimension 0, may hold values from 0 to 4, as said below
Outputs:
- hess_vec: float32 [64, 4096], P(None, ('parts', 'blk', 'grp')), parts along dimension 1
- residual: float32 [64, 4096], P(None, ('parts', 'blk', 'grp')), parts along dimension 1
- inner: float32 [4], P('parts'), parts along dimension 0
There are 2 independent parts, one for each index of `parts`. A program takes and returns all parts, laid end to end along the dimension named above; each array names one. Nothing has to cross between parts.
Inputs may be any that keep to these rules, and one draw needn't show every extreme that they name: counts is symmetric.
All inputs are finite; a program needn't handle non-finite values.
Results may differ from a plain program's by a relative error of at most 0.0003.
Values sent between devices are 32-bit elements; how exact they have to be, the bound alone decides.
A program may use at most 128 MiB of HBM per device.

v0:
```python
import jax
import jax.numpy as jnp
from jax import lax
from jax.sharding import PartitionSpec as P


def local(factors, tangent, counts):
    rows = counts.shape[0]
    nodes = counts.shape[1]
    scale = 1.0 / jnp.sqrt(jnp.float32(nodes))
    highest = lax.Precision.HIGHEST
    contract = (((0,), (0,)), ((), ()))
    right = (((1,), (1,)), ((), ()))
    row_start = (lax.axis_index("blk") * lax.axis_size("grp") + lax.axis_index("grp")) * rows
    row_ids = row_start + jnp.arange(rows, dtype=jnp.int32)[:, None]
    group_u, group_v = (
        lax.all_gather(factors, "grp", axis=1, tiled=True),
        lax.all_gather(tangent, "grp", axis=1, tiled=True),
    )
    piece_u = lax.all_gather(group_u, "blk", axis=1, tiled=True)
    piece_v = lax.all_gather(group_v, "blk", axis=1, tiled=True)
    width = piece_u.shape[1]
    eta = lax.dot_general(factors, piece_u, contract, precision=highest)
    deta = lax.dot_general(factors, piece_v, contract, precision=highest) + lax.dot_general(
        tangent, piece_u, contract, precision=highest
    )
    col_ids = jnp.arange(width, dtype=jnp.int32)[None, :]
    keep = row_ids != col_ids
    rate = jnp.where(keep, jnp.exp(eta), jnp.float32(0.0))
    weight = rate * deta
    tile_counts = counts.astype(jnp.float32)
    slack = jnp.where(keep, tile_counts - rate, jnp.float32(0.0))
    hess_acc = lax.dot_general(piece_u, weight, right, precision=highest)
    resid_acc = lax.dot_general(piece_u, slack - weight, right, precision=highest)
    hess_acc, resid_acc = (hess_acc, resid_acc)
    hess_vec = hess_acc * scale
    residual = resid_acc * scale
    sum_sq, sum_curv = lax.psum(
        (jnp.sum(residual * residual), jnp.sum(tangent * hess_vec)), ("blk", "grp")
    )
    inner = jnp.stack([sum_sq, sum_curv])
    return (hess_vec, residual, inner)


def solution(mesh):
    return jax.shard_map(
        local,
        mesh=mesh,
        in_specs=(
            P(None, ("parts", "blk", "grp")),
            P(None, ("parts", "blk", "grp")),
            P(("parts", "blk", "grp"), None),
        ),
        out_specs=(P(None, ("parts", "blk", "grp")), P(None, ("parts", "blk", "grp")), P("parts")),
        check_vma=False,
    )
```

profile of v0, /device:TPU:0, one launch (start us, length us, event | category | flops | bytes accessed | tf_op | source)
XLA Modules:
  0.0 85.9 jit_solution(17943244656120877728)
XLA Ops:
  0.6 0.0 copy-start.1
  0.7 6.7 %all_gather.12 = f32[64,512]{1,0:T(8,128)S(1)} all-gather(f32[64,128]{1,0:T(8,128)} %param.3), channel_id=1, replica_groups=mesh['parts'=2,'blk'=4,'grp'=4] {'grp'}, dimensions={1}, use_global_device_ids=true | all-gather | bytes 163840 | tf_op jit(solution)/shard_map/all_gather | solution.py:17
  7.4 0.0 copy-done.1
  7.4 5.6 %all_gather.14 = f32[64,512]{1,0:T(8,128)S(1)} all-gather(f32[64,128]{1,0:T(8,128)S(1)} %copy-done.1), channel_id=1, replica_groups=mesh['parts'=2,'blk'=4,'grp'=4] {'grp'}, dimensions={1}, use_global_device_ids=true | all-gather | bytes 163840 | tf_op jit(solution)/shard_map/all_gather | solution.py:18
  12.9 16.6 %all_gather.13 = f32[64,2048]{1,0:T(8,128)S(1)} all-gather(f32[64,512]{1,0:T(8,128)S(1)} %all_gather.12), channel_id=1, replica_groups=mesh['parts'=2,'blk'=4,'grp'=4] {'blk'}, dimensions={1}, use_global_device_ids=true | all-gather | bytes 655360 | tf_op jit(solution)/shard_map/all_gather | solution.py:20
  29.5 0.0 copy-start.2
  29.5 16.0 %all_gather.15 = f32[64,2048]{1,0:T(8,128)S(1)} all-gather(f32[64,512]{1,0:T(8,128)S(1)} %all_gather.14), channel_id=1, replica_groups=mesh['parts'=2,'blk'=4,'grp'=4] {'blk'}, dimensions={1}, use_global_device_ids=true | all-gather | bytes 655360 | tf_op jit(solution)/shard_map/all_gather | solution.py:21
  45.5 0.0 copy-done.2
  45.5 1.0 %fusion.11 = f32[128,2048]{1,0:T(8,128)S(1)} fusion(f32[64,128]{1,0:T(8,128)S(1)} %copy-done.2, f32[64,2048]{1,0:T(8,128)S(1)} %all_gather.15), kind=kOutput, calls=%fused_computation.20 | convolution fusion | flops 201326592 | bytes 1605632 | tf_op jit(solution)/shard_map/dot_general | solution.py:24
  46.6 1.1 %fusion.1 = f32[128,2048]{1,0:T(8,128)S(1)} fusion(f32[64,128]{1,0:T(8,128)S(1)} %copy-done.2, f32[64,2048]{1,0:T(8,128)S(1)} %all_gather.13, s32[128]{0:T(128)S(1)} %iota_add_fusion), kind=kOutput, calls=%fused_computation.3 | convolution fusion | flops 201850880 | bytes 1606144 | tf_op jit(solution)/shard_map/dot_general | solution.py:23
  47.7 0.0 copy-start
  47.7 1.1 %fusion = f32[128,2048]{1,0:T(8,128)S(1)} fusion(f32[128,2048]{1,0:T(8,128)S(1)} %fusion.1, f32[128,2048]{1,0:T(8,128)S(1)} %fusion.11, f32[64,128]{1,0:T(8,128)S(1)} %copy-done.1, f32[64,2048]{1,0:T(8,128)S(1)} %all_gather.13), kind=kOutput, calls=%fused_computation.1 | convolution fusion | flops 201850880 | bytes 3702784 | tf_op jit(solution)/shard_map/dot_general | solution.py:24
  48.8 0.2 copy-done
  48.9 2.7 %multiply_reduce_fusion.1 = (f32[]{:T(128)}, f32[64,128]{1,0:T(8,128)}) fusion(f32[64,2048]{1,0:T(8,128)S(1)} %all_gather.13, f32[128,2048]{1,0:T(8,128)S(1)} %fusion, f32[128,2048]{1,0:T(8,128)S(1)} %fusion.1, s32[128,2048]{1,0:T(8,128)S(1)} %copy-done, s32[128]{0:T(128)S(1)} %iota_add_fusion), kind=kOutput, calls=%fused_computation.16 | convolution fusion | flops 202661888 | bytes 3703300 | tf_op jit(solution)/shard_map/dot_general | solution.py:34
  51.6 2.4 %multiply_reduce_fusion = (f32[]{:T(128)}, f32[64,128]{1,0:T(8,128)}) fusion(f32[64,128]{1,0:T(8,128)S(1)} %copy-done.1, f32[128,2048]{1,0:T(8,128)S(1)} %fusion, f32[64,2048]{1,0:T(8,128)S(1)} %all_gather.13), kind=kOutput, calls=%fused_computation.15 | convolution fusion | flops 201351168 | bytes 1638404 | tf_op jit(solution)/shard_map/dot_general | solution.py:33
  54.0 30.1 %all-reduce = (f32[1]{0:T(128)}, f32[1]{0:T(128)}) all-reduce(f32[1]{0:T(128)} %bitcast.3, f32[1]{0:T(128)} %bitcast.2), channel_id=1, replica_groups=mesh['parts'=2,'blk'=4,'grp'=4] {'blk','grp'}, use_global_device_ids=true, to_apply=%region_3.4 | all-reduce | flops 2 | bytes 16 | tf_op jit(solution)/shard_map/psum | solution.py:38
  84.2 1.8 %pad_maximum_fusion = f32[2]{0:T(128)} fusion(f32[1]{0:T(128)} %get-tuple-element.3, f32[1]{0:T(128)} %get-tuple-element.4), kind=kLoop, calls=%fused_computation.17 | loop fusion | flops 2 | bytes 16 | tf_op jit(solution)/shard_map/stack | solution.py:41
  (1 shorter events, 0.0 us)
Async XLA Ops:
  0.6 6.7 %copy-start.1 = (f32[64,128]{1,0:T(8,128)S(1)}, f32[64,128]{1,0:T(8,128)}, u32[]{:S(2)}) copy-start(f32[64,128]{1,0:T(8,128)} %param.4) | copy-start | bytes 98308
  29.5 16.0 %copy-start.2 = (f32[64,128]{1,0:T(8,128)S(1)}, f32[64,128]{1,0:T(8,128)}, u32[]{:S(2)}) copy-start(f32[64,128]{1,0:T(8,128)} %param.3) | copy-start | bytes 98308
  47.7 1.2 %copy-start = (s32[128,2048]{1,0:T(8,128)S(1)}, s32[128,2048]{1,0:T(8,128)}, u32[]{:S(2)}) copy-start(s32[128,2048]{1,0:T(8,128)} %param.5) | copy-start | bytes 3145732
where the time goes:
time: 86.3 us; the launch traced here: 85.9 us
  blocking collectives  75 us (87%)
  matrix products  8.3 us (10%)
  other arithmetic  1.78 us (2%)
    psum x1, blocking collectives, local(): lax.psum((jnp.sum(residual * residual), jnp.sum(tangent * hess_vec)), ('b...  30.1 us
    all_gather x1, blocking collectives, local(): piece_u = lax.all_gather(group_u, 'blk', axis=1, tiled=True)  16.6 us
    all_gather x1, blocking collectives, local(): piece_v = lax.all_gather(group_v, 'blk', axis=1, tiled=True)  16 us
    all_gather x1, blocking collectives, local(): lax.all_gather(factors, 'grp', axis=1, tiled=True)  6.69 us
    all_gather x1, blocking collectives, local(): lax.all_gather(tangent, 'grp', axis=1, tiled=True)  5.58 us
    dot_general x1, matrix products, local(): lax.dot_general(piece_u, slack - weight, right, precision=highest)  2.69 us
    dot_general x1, matrix products, local(): hess_acc = lax.dot_general(piece_u, weight, right, precision=highest)  2.41 us
    another operation x1, other arithmetic, local(): inner = jnp.stack([sum_sq, sum_curv])  1.78 us

commit v1 on v0

--- a/solution.py
+++ b/solution.py
@@ -1,7 +1,40 @@
+import functools
 import jax
 import jax.numpy as jnp
 from jax import lax
 from jax.sharding import PartitionSpec as P
+
+
+def clusters_finish(base_x, axis_name, d_out):
+    z2 = lax.psum(1, axis_name)
+    clean = lax.axis_index(axis_name)
+    d_next, z, local_next = (z2, clean, base_x.shape[d_out])
+    steps_seen = []
+    for j0 in range(d_next):
+        steps_seen.append((j0, (j0 + 1) % d_next))
+    samples = []
+    for j0 in range(d_next):
+        samples.append((j0, (j0 - 1) % d_next))
+    next_value = jnp.zeros(
+        (*base_x.shape[:d_out], d_next * local_next, *base_x.shape[d_out + 1 :]), base_x.dtype
+    )
+    next_value = lax.dynamic_update_slice_in_dim(next_value, base_x, z * local_next, axis=d_out)
+    all_rows = out_arr = base_x
+    v1 = d_next // 2
+    for to_i in range(1, v1 + 1):
+        all_rows = lax.ppermute(all_rows, axis_name=axis_name, perm=steps_seen)
+        next_value = lax.dynamic_update_slice_in_dim(
+            next_value, all_rows, (z - to_i) % d_next * local_next, axis=d_out
+        )
+        if to_i < d_next - v1:
+            out_arr = lax.ppermute(out_arr, axis_name=axis_name, perm=samples)
+            next_value = lax.dynamic_update_slice_in_dim(
+                next_value, out_arr, (z + to_i) % d_next * local_next, axis=d_out
+            )
+    return next_value
+
+
+draw_loops_on = functools.partial(clusters_finish, axis_name="grp", d_out=1)
 
 
 def local(factors, tangent, counts):
@@ -13,10 +46,7 @@
     right = (((1,), (1,)), ((), ()))
     row_start = (lax.axis_index("blk") * lax.axis_size("grp") + lax.axis_index("grp")) * rows
     row_ids = row_start + jnp.arange(rows, dtype=jnp.int32)[:, None]
-    group_u, group_v = (
-        lax.all_gather(factors, "grp", axis=1, tiled=True),
-        lax.all_gather(tangent, "grp", axis=1, tiled=True),
-    )
+    group_u, group_v = (draw_loops_on(factors), lax.all_gather(tangent, "grp", axis=1, tiled=True))
     piece_u = lax.all_gather(group_u, "blk", axis=1, tiled=True)
     piece_v = lax.all_gather(group_v, "blk", axis=1, tiled=True)
     width = piece_u.shape[1]

time: 86.3 us -> 87.3 us (1.012)
  blocking collectives: 75 us -> 68.6 us
  waiting for transfers between devices: 0 us -> 3.29 us
  starting transfers between devices: 0 us -> 2.55 us
  matrix products: 8.3 us -> 9.54 us
    all_gather x1 -> x0, blocking collectives: 6.69 us -> none  [local(): lax.all_gather(factors, 'grp', axis=1, tiled=True)]
    ppermute x0 -> x3, waiting for transfers between devices: none -> 3.29 us  [the longest x2 3.28 us: clusters_finish(): all_rows = lax.ppermute(all_rows, axis_name=axis_name, perm=steps_seen)]
    ppermute x0 -> x3, starting transfers between devices: none -> 2.55 us  [the longest x1 1.99 us: clusters_finish(): out_arr = lax.ppermute(out_arr, axis_name=axis_name, perm=samples)]
    all_gather x1, blocking collectives: 16.6 us -> 15.6 us  [local(): piece_u = lax.all_gather(group_u, 'blk', axis=1, tiled=True)]
  transfers between devices with their start and end apart: 0 -> 3, of which waited for: 0 -> 1; matrix products, arithmetic and copies ran while one was open for 0% -> 3% of each run, Pallas kernels for 0% -> 0%
where the time goes in v1:
time: 87.3 us; the launch traced here: 87 us
  blocking collectives  68.6 us (79%)
  matrix products  9.54 us (11%)
  waiting for transfers between devices  3.29 us (4%)
  starting transfers between devices  2.55 us (3%)
  other arithmetic  1.85 us (2%)
    psum x1, blocking collectives, local(): lax.psum((jnp.sum(residual * residual), jnp.sum(tangent * hess_vec)), ('b...  30.2 us
    all_gather x1, blocking collectives, local(): piece_v = lax.all_gather(group_v, 'blk', axis=1, tiled=True)  16.9 us
    all_gather x1, blocking collectives, local(): piece_u = lax.all_gather(group_u, 'blk', axis=1, tiled=True)  15.6 us
    all_gather x1, blocking collectives, local(): lax.all_gather(tangent, 'grp', axis=1, tiled=True)  5.98 us
    ppermute x2, waiting for transfers between devices, clusters_finish(): all_rows = lax.ppermute(all_rows, axis_name=axis_name, perm=steps_seen)  3.28 us
    dot_general x1, matrix products, local(): lax.dot_general(piece_u, slack - weight, right, precision=highest)  2.15 us
    ppermute x1, starting transfers between devices, clusters_finish(): out_arr = lax.ppermute(out_arr, axis_name=axis_name, perm=samples)  1.99 us
    dot_general x1, matrix products, local(): hess_acc = lax.dot_general(piece_u, weight, right, precision=highest)  1.95 us
  transfers between devices with their start and end apart: 3, of which 1 were waited for; matrix products, arithmetic and copies ran while one was open for 3% of the time, Pallas kernels for 0%

profile of v1, /device:TPU:0, one launch (start us, length us, event | category | flops | bytes accessed | tf_op | source)
XLA Modules:
  0.0 87.0 jit_solution(16059933205235583533)
XLA Ops:
  0.6 0.5 collective-permute-start
  1.1 2.0 %collective-permute-start.1 = (f32[64,128]{1,0:T(8,128)}, f32[64,128]{1,0:T(8,128)S(1)}, u32[]{:S(2)}, u32[]{:S(2)}) collective-permute-start(f32[64,128]{1,0:T(8,128)} %param.3), channel_id=1, source_target_pairs={{0,3},{1,0},{2,1},{3,2},{4,7},{5,4},{6,5},{7,6},{8,11},{9,8},{10,9... | collective-permute-start | bytes 98312 | tf_op jit(solution)/shard_map/ppermute | solution.py:30
  3.1 6.0 %all_gather.10 = f32[64,512]{1,0:T(8,128)S(1)} all-gather(f32[64,128]{1,0:T(8,128)} %param.4), channel_id=1, replica_groups=mesh['parts'=2,'blk'=4,'grp'=4] {'grp'}, dimensions={1}, use_global_device_ids=true | all-gather | bytes 163840 | tf_op jit(solution)/shard_map/all_gather | solution.py:49
  9.1 0.0 copy-start.2
  9.1 16.9 %all_gather.11 = f32[64,2048]{1,0:T(8,128)S(1)} all-gather(f32[64,512]{1,0:T(8,128)S(1)} %all_gather.10), channel_id=1, replica_groups=mesh['parts'=2,'blk'=4,'grp'=4] {'blk'}, dimensions={1}, use_global_device_ids=true | all-gather | bytes 655360 | tf_op jit(solution)/shard_map/all_gather | solution.py:51
  26.0 0.0 copy-done.2
  26.0 0.0 copy-start
  26.0 1.8 %fusion.11 = f32[128,2048]{0,1:T(8,128)S(1)} fusion(f32[64,128]{1,0:T(8,128)S(1)} %copy-done.2, f32[64,2048]{1,0:T(8,128)S(1)} %all_gather.11), kind=kOutput, calls=%fused_computation.24 | convolution fusion | flops 201326592 | bytes 1605632 | tf_op jit(solution)/shard_map/dot_general | solution.py:54
  27.9 0.0 copy-done
  27.9 0.3 copy.7
  28.3 0.0 collective-permute-done
  28.3 0.1 collective-permute-start.2
  28.4 0.0 collective-permute-done.1
  28.4 3.3 %collective-permute-done.2 = f32[64,128]{1,0:T(8,128)S(1)} collective-permute-done((f32[64,128]{1,0:T(8,128)S(1)}, f32[64,128]{1,0:T(8,128)S(1)}, u32[]{:S(2)}, u32[]{:S(2)}) %collective-permute-start.2) | collective-permute-done | bytes 32800 | tf_op jit(solution)/shard_map/ppermute | solution.py:25
  31.7 15.6 %all_gather.9 = f32[64,2048]{1,0:T(8,128)S(1)} all-gather(f32[64,512]{1,0:T(8,128)S(1)} %constant_dynamic-update-slice_fusion), channel_id=1, replica_groups=mesh['parts'=2,'blk'=4,'grp'=4] {'blk'}, dimensions={1}, use_global_device_ids=true | all-gather | bytes 655360 | tf_op jit(solution)/shard_map/all_gather | solution.py:50
  47.3 0.0 copy-start.1
  47.3 1.8 %fusion.3 = f32[128,2048]{0,1:T(8,128)S(1)} fusion(f32[64,2048]{1,0:T(8,128)S(1)} %all_gather.9, f32[64,128]{1,0:T(8,128)S(1)} %copy-done.2, s32[128]{0:T(128)S(1)} %iota_add_fusion), kind=kOutput, calls=%fused_computation.5 | convolution fusion | flops 201850880 | bytes 1606144 | tf_op jit(solution)/shard_map/dot_general | solution.py:53
  49.1 0.0 copy-done.1
  49.1 1.8 %fusion.1 = f32[128,2048]{0,1:T(8,128)S(1)} fusion(f32[128,2048]{0,1:T(8,128)S(1)} %fusion.3, f32[128,2048]{0,1:T(8,128)S(1)} %fusion.11, f32[64,2048]{1,0:T(8,128)S(1)} %all_gather.9, f32[64,128]{1,0:T(8,128)S(1)} %copy-done.1), kind=kOutput, calls=%fused_computation.2 | convolution fusion | flops 201850880 | bytes 3702784 | tf_op jit(solution)/shard_map/dot_general | solution.py:54
  50.9 2.0 %multiply_reduce_fusion = (f32[]{:T(128)}, f32[64,128]{1,0:T(8,128)}) fusion(f32[64,128]{1,0:T(8,128)S(1)} %copy-done.1, f32[64,2048]{1,0:T(8,128)S(1)} %all_gather.9, f32[128,2048]{0,1:T(8,128)S(1)} %fusion.1), kind=kOutput, calls=%fused_computation.15 | convolution fusion | flops 201351168 | bytes 1638404 | tf_op jit(solution)/shard_map/dot_general | solution.py:63
  52.9 2.2 %multiply_reduce_fusion.1 = (f32[]{:T(128)}, f32[64,128]{1,0:T(8,128)}) fusion(f32[64,2048]{1,0:T(8,128)S(1)} %all_gather.9, f32[128,2048]{0,1:T(8,128)S(1)} %fusion.1, f32[128,2048]{0,1:T(8,128)S(1)} %fusion.3, s32[128,2048]{0,1:T(8,128)S(1)} %copy.7, s32[128]{0:T(128)S(1)} %iota_add_fusion), kind=kOutput, calls=%fused_computation.16 | convolution fusion | flops 202661888 | bytes 3703300 | tf_op jit(solution)/shard_map/dot_general | solution.py:64
  55.0 30.2 %all-reduce = (f32[1]{0:T(128)}, f32[1]{0:T(128)}) all-reduce(f32[1]{0:T(128)} %bitcast.3, f32[1]{0:T(128)} %bitcast.2), channel_id=1, replica_groups=mesh['parts'=2,'blk'=4,'grp'=4] {'blk','grp'}, use_global_device_ids=true, to_apply=%region_3.4 | all-reduce | flops 2 | bytes 16 | tf_op jit(solution)/shard_map/psum | solution.py:68
  85.2 1.8 %pad_maximum_fusion = f32[2]{0:T(128)} fusion(f32[1]{0:T(128)} %get-tuple-element.3, f32[1]{0:T(128)} %get-tuple-element.4), kind=kLoop, calls=%fused_computation.21 | loop fusion | flops 2 | bytes 16 | tf_op jit(solution)/shard_map/stack | solution.py:71
  (6 shorter events, 0.0 us)
Async XLA Ops:
  0.6 27.6 %collective-permute-start = (f32[64,128]{1,0:T(8,128)}, f32[64,128]{1,0:T(8,128)S(1)}, u32[]{:S(2)}, u32[]{:S(2)}) collective-permute-start(f32[64,128]{1,0:T(8,128)} %param.3), channel_id=1, source_target_pairs={{0,1},{1,2},{2,3},{3,0},{4,5},{5,6},{6,7},{7,4},{8,9},{9,10},{10,1... | collective-permute-start | bytes 98312 | tf_op jit(solution)/shard_map/ppermute | solution.py:25
  1.1 27.2 %collective-permute-start.1 = (f32[64,128]{1,0:T(8,128)}, f32[64,128]{1,0:T(8,128)S(1)}, u32[]{:S(2)}, u32[]{:S(2)}) collective-permute-start(f32[64,128]{1,0:T(8,128)} %param.3), channel_id=1, source_target_pairs={{0,3},{1,0},{2,1},{3,2},{4,7},{5,4},{6,5},{7,6},{8,11},{9,8},{10,9... | collective-permute-start | bytes 98312 | tf_op jit(solution)/shard_map/ppermute | solution.py:30
  9.1 16.9 %copy-start.2 = (f32[64,128]{1,0:T(8,128)S(1)}, f32[64,128]{1,0:T(8,128)}, u32[]{:S(2)}) copy-start(f32[64,128]{1,0:T(8,128)} %param.3) | copy-start | bytes 98308
  26.0 1.9 %copy-start = (s32[128,2048]{1,0:T(8,128)S(1)}, s32[128,2048]{1,0:T(8,128)}, u32[]{:S(2)}) copy-start(s32[128,2048]{1,0:T(8,128)} %param.5) | copy-start | bytes 3145732
  28.3 3.4 %collective-permute-start.2 = (f32[64,128]{1,0:T(8,128)S(1)}, f32[64,128]{1,0:T(8,128)S(1)}, u32[]{:S(2)}, u32[]{:S(2)}) collective-permute-start(f32[64,128]{1,0:T(8,128)S(1)} %collective-permute-done), channel_id=1, source_target_pairs={{0,1},{1,2},{2,3},{3,0},{4,5},{5,6},{6,7},{7,4},{8,9},{9,10},{10,1... | collective-permute-start | bytes 98312 | tf_op jit(solution)/shard_map/ppermute | solution.py:25
  47.3 1.8 %copy-start.1 = (f32[64,128]{1,0:T(8,128)S(1)}, f32[64,128]{1,0:T(8,128)}, u32[]{:S(2)}) copy-start(f32[64,128]{1,0:T(8,128)} %param.4) | copy-start | bytes 98308
